TPU v7x, 32 devices: a whole 2x2x4 slice. The times are simulated.
32 devices in a mesh: row: 4 (over z), col: 8 (over y, x, core).
Axes of the slice: x: 2, y: 2, z: 4, core: 2. Of those that a mesh axis runs over, the one named last changes fastest.
Arguments:
- cotangent: float32 [4096, 8192], P('row', 'col'), may hold values from -6 to 6
- whitened: float32 [4096, 8192], P('row', 'col'), may hold values from -0.0625 to 0.0625
- panel_rows: float32 [4, 256, 4096], P(None, None, 'row'), may hold values from -0.375 to 0.375
- diag_inverse: float32 [4, 256, 256], replicated, as said below
Outputs:
- adjoint_rhs: float32 [4096, 8192], P('row', 'col')
- factor_grad: float32 [4, 256, 4096], P(None, 'col', 'row')
Inputs may be any that keep to these rules, and one draw needn't show every extreme that they name: `diag_inverse`: each block is lower triangular with diagonal entries between 0.5 and 1.5.
All inputs are finite; a program needn't handle non-finite values.
Results may differ from a plain program's by a relative error of at most 0.00017.
Values sent between devices are 32-bit elements; how exact they have to be, the bound alone decides.
A program may use at most 128 MiB of HBM per device.

v0:
```python
import jax
import jax.numpy as jnp
from jax import lax
from jax.sharding import PartitionSpec as P


def broadcast(array, axis, root):
    mine = lax.axis_index(axis) == root
    return lax.psum(jnp.where(mine, array, jnp.zeros_like(array)), axis)


def grad_mask(count, natural, within, target):
    inner = jnp.arange(count, dtype=jnp.int32)
    return (natural[None, :] < target) | (natural[None, :] == target) & (
        inner[:, None] >= within[None, :]
    )


def body(cotangent, whitened, panel_rows, diag_inverse):
    hi = lax.Precision.HIGHEST
    n_row = lax.axis_size("row")
    rows_dev = cotangent.shape[0]
    width = diag_inverse.shape[1]
    panel_count = panel_rows.shape[0]
    blocks = rows_dev // width * n_row
    device = lax.axis_index("row")
    local = jnp.arange(rows_dev, dtype=jnp.int32)
    natural = local // width * n_row + device
    within = local % width
    residual = cotangent
    terms = []
    for p in range(panel_count):
        target = blocks - 1 - p
        root = n_row - 1 - p
        own = residual[rows_dev - width :]
        solved = jnp.dot(diag_inverse[p].T, own, precision=hi, preferred_element_type=jnp.float32)
        solved = broadcast(solved, "row", root)
        masked = jnp.where((natural < target)[None, :], panel_rows[p], 0.0)
        update = lax.dot_general(
            masked,
            solved,
            (((0,), (0,)), ((), ())),
            precision=hi,
            preferred_element_type=jnp.float32,
        )
        residual = residual - update
        tail = jnp.where(device == root, solved, residual[rows_dev - width :])
        residual = jnp.concatenate([residual[: rows_dev - width], tail], 0)
        partial_term = lax.dot_general(
            solved,
            whitened,
            (((1,), (1,)), ((), ())),
            precision=hi,
            preferred_element_type=jnp.float32,
        )
        terms.append(jnp.where(grad_mask(width, natural, within, target), -partial_term, 0.0))
    factor_grad = lax.psum_scatter(jnp.stack(terms), "col", scatter_dimension=1, tiled=True)
    return (residual, factor_grad)


def solution(mesh):
    return jax.shard_map(
        body,
        mesh=mesh,
        in_specs=(P("row", "col"), P("row", "col"), P(None, None, "row"), P()),
        out_specs=(P("row", "col"), P(None, "col", "row")),
        check_vma=False,
    )
```

profile of v0, /device:TPU:0, one launch (start us, length us, event | category | flops | bytes accessed | tf_op | source)
XLA Modules:
  0.0 321.2 jit_solution(1200197251109899264)
XLA Ops:
  7.2 3.3 %convolution_select_fusion.3 = f32[256,1024]{1,0:T(8,128)} fusion(f32[1024,1024]{1,0:T(8,128)} %param.4, pred[]{:T(512)S(6)} %eq.50, f32[4,256,256]{2,1,0:T(8,128)} %param.7), kind=kOutput, calls=%fused_computation.12 | convolution fusion | flops 805568512 | bytes 2359297 | tf_op jit(solution)/shard_map/dot_general | solution.py:36
  10.6 54.9 %all-reduce.5.cloned.1.call-done = f32[256,1024]{1,0:T(8,128)} async-done(((f32[256,1024]{1,0:T(8,128)}), f32[256,1024]{1,0:T(8,128)}) %all-reduce.5.cloned.1.call-update) | async-done | bytes 1048592 | tf_op jit(solution)/shard_map/psum | solution.py:9
  65.6 6.7 %convolution_subtract_fusion = f32[1024,1024]{1,0:T(8,128)S(1)} fusion(f32[1024,1024]{1,0:T(8,128)} %param.4, f32[256,1024]{1,0:T(8,128)} %all-reduce.5.cloned.1.call-done, f32[4,256,1024]{2,1,0:T(8,128)} %param.6, pred[1024]{0:T(1024)(128)(4,1)S(1)} %fusion.56), kind=kOutput, calls=%fused_computation.5 | convolution fusion | flops 3222536192 | bytes 10486784 | tf_op jit(solution)/shard_map/dot_general | solution.py:39
  72.3 2.0 copy-done.3
  74.4 1.0 copy-done.12
  75.4 3.0 fusion.2
  78.6 51.2 %all-reduce.7.cloned.1.call-done = f32[256,1024]{1,0:T(8,128)} async-done(((f32[256,1024]{1,0:T(8,128)}), f32[256,1024]{1,0:T(8,128)}) %all-reduce.7.cloned.1.call-update) | async-done | bytes 1048592 | tf_op jit(solution)/shard_map/psum | solution.py:9
  129.8 5.8 %maximum_subtract_fusion = f32[1024,1024]{1,0:T(8,128)S(1)} fusion(f32[256,1024]{1,0:T(8,128)} %copy-done.12, f32[768,1024]{1,0:T(8,128)S(1)} %slice-done.2, f32[256,1024]{1,0:T(8,128)} %all-reduce.7.cloned.1.call-done, f32[4,256,1024]{2,1,0:T(8,128)} %param.6, pred[1024]{0:T(1024)(128)(4,1)S(1)} %fusion.55), kind=kOutput, calls=%fused_computation | convolution fusion | flops 3223584768 | bytes 10486784 | tf_op jit(solution)/shard_map/dot_general | solution.py:39
  135.6 2.0 copy-done.2
  138.7 3.1 fusion.1
  142.1 51.0 %all-reduce.9.cloned.1.call-done = f32[256,1024]{1,0:T(8,128)} async-done(((f32[256,1024]{1,0:T(8,128)}), f32[256,1024]{1,0:T(8,128)}) %all-reduce.9.cloned.1.call-update) | async-done | bytes 1048592 | tf_op jit(solution)/shard_map/psum | solution.py:9
  193.1 5.8 %maximum_subtract_fusion.1 = f32[1024,1024]{1,0:T(8,128)S(1)} fusion(f32[256,1024]{1,0:T(8,128)} %copy-done.11, f32[768,1024]{1,0:T(8,128)S(1)} %slice-done.1, f32[256,1024]{1,0:T(8,128)} %all-reduce.9.cloned.1.call-done, f32[4,256,1024]{2,1,0:T(8,128)} %param.6, pred[1024]{0:T(1024)(128)(4,1)S(1)} %fusion.54), kind=kOutput, calls=%fused_computation.1 | convolution fusion | flops 3223584768 | bytes 10486784 | tf_op jit(solution)/shard_map/dot_general | solution.py:39
  198.9 2.0 copy-done.1
  201.1 3.1 fusion
  204.3 7.1 %fusion.10 = f32[1,256,1024]{2,1,0:T(8,128)} fusion(f32[256,1024]{1,0:T(8,128)S(1)} %copy-done.5, f32[1024,1024]{1,0:T(8,128)} %param.5, s32[1024]{0:T(1024)S(1)} %fusion.40, pred[1024]{0:T(1024)(128)(4,1)S(1)} %get-tuple-element.5, pred[1024]{0:T(1024)(128)(4,1)S(1)} %fusion.56), kind=kOutput, calls=%fused_computation.24 | convolution fusion | flops 3222536192 | bytes 6297600 | tf_op jit(solution)/shard_map/dot_general | solution.py:49
  211.4 4.8 %fusion.8 = f32[1,256,1024]{2,1,0:T(8,128)} fusion(f32[256,1024]{1,0:T(8,128)S(1)} %copy-done.7, f32[1024,1024]{1,0:T(8,128)S(1)} %copy-done, s32[1024]{0:T(1024)S(1)} %fusion.40, pred[1024]{0:T(1024)(128)(4,1)S(1)} %get-tuple-element.4, pred[1024]{0:T(1024)(128)(4,1)S(1)} %fusion.55), kind=kOutput, calls=%fused_computation.21 | convolution fusion | flops 3222536192 | bytes 6297600 | tf_op jit(solution)/shard_map/dot_general | solution.py:49
  216.1 4.8 %fusion.6 = f32[1,256,1024]{2,1,0:T(8,128)} fusion(f32[256,1024]{1,0:T(8,128)S(1)} %copy-done.10, f32[1024,1024]{1,0:T(8,128)S(1)} %copy-done, s32[1024]{0:T(1024)S(1)} %fusion.40, pred[1024]{0:T(1024)(128)(4,1)S(1)} %get-tuple-element.3, pred[1024]{0:T(1024)(128)(4,1)S(1)} %fusion.54), kind=kOutput, calls=%fused_computation.18 | convolution fusion | flops 3222536192 | bytes 6297600 | tf_op jit(solution)/shard_map/dot_general | solution.py:49
  220.9 34.6 %all-reduce.11.cloned.1.call-done = f32[256,1024]{1,0:T(8,128)} async-done(((f32[256,1024]{1,0:T(8,128)}), f32[256,1024]{1,0:T(8,128)}) %all-reduce.11.cloned.1.call-update) | async-done | bytes 1048592 | tf_op jit(solution)/shard_map/psum | solution.py:9
  255.5 6.2 %fusion.4 = f32[1,256,1024]{2,1,0:T(8,128)S(1)} fusion(f32[256,1024]{1,0:T(8,128)} %all-reduce.11.cloned.1.call-done, f32[1024,1024]{1,0:T(8,128)} %param.5, s32[1024]{0:T(1024)S(1)} %fusion.40, pred[1024]{0:T(1024)(128)(4,1)S(1)} %get-tuple-element.2, pred[1024]{0:T(1024)(128)(4,1)S(1)} %fusion.53), kind=kOutput, calls=%fused_computation.15 | convolution fusion | flops 3222536192 | bytes 6297600 | tf_op jit(solution)/shard_map/dot_general | solution.py:49
  261.8 2.3 pad_maximum_fusion.1
  264.1 1.9 slice-done
  266.2 5.0 %maximum_subtract_fusion.2 = f32[1024,1024]{1,0:T(8,128)S(1)} fusion(f32[256,1024]{1,0:T(8,128)S(1)} %slice_select_fusion.1, f32[768,1024]{1,0:T(8,128)S(1)} %slice-done, f32[256,1024]{1,0:T(8,128)S(1)} %copy-done.8, f32[4,256,1024]{2,1,0:T(8,128)} %param.6, pred[1024]{0:T(1024)(128)(4,1)S(1)} %fusion.53), kind=kOutput, calls=%fused_computation.2 | convolution fusion | flops 3223584768 | bytes 10486784 | tf_op jit(solution)/shard_map/dot_general | solution.py:39
  271.8 2.3 pad_maximum_fusion
  274.2 40.5 %reduce-scatter.2.cloned.1.call-done = f32[4,32,1024]{2,1,0:T(8,128)} async-done(((f32[4,256,1024]{2,1,0:T(8,128)}), f32[4,32,1024]{2,1,0:T(8,128)}) %reduce-scatter.2.cloned.1.call-update) | async-done | bytes 524304 | tf_op jit(solution)/shard_map/reduce_scatter | solution.py:57
  (55 shorter events, 2.8 us)
Async XLA Ops:
  7.2 58.4 %all-reduce.5.cloned.1.call-start = ((), (), s32[]{:S(2)}) async-start(), calls=%async_computation.1 | async-start | bytes 2097152 | tf_op jit(solution)/shard_map/psum | solution.py:9
  10.6 119.2 %all-reduce.7.cloned.1.call-start = ((), (), s32[]{:S(2)}) async-start(), calls=%async_computation.2 | async-start | bytes 2097152 | tf_op jit(solution)/shard_map/psum | solution.py:9
  65.6 8.7 %copy-start.4 = (f32[256,1024]{1,0:T(8,128)S(1)}, f32[256,1024]{1,0:T(8,128)}, u32[]{:S(2)}) copy-start(f32[256,1024]{1,0:T(8,128)} %all-reduce.5.cloned.1.call-done) | copy-start | bytes 3145732
  72.3 2.0 copy-start.3
  74.4 1.0 copy-start.12
  78.5 51.3 %slice-start.2 = ((f32[1024,1024]{1,0:T(8,128)}), f32[768,1024]{1,0:T(8,128)S(1)}, s32[]{:S(2)}) async-start(f32[1024,1024]{1,0:T(8,128)} %copy-done.3), calls=%async_computation.8 | async-start | bytes 6291456 | tf_op jit(solution)/shard_map/slice | solution.py:48
  78.5 114.6 %all-reduce.9.cloned.1.call-start = ((), (), s32[]{:S(2)}) async-start(), calls=%async_computation.3 | async-start | bytes 2097152 | tf_op jit(solution)/shard_map/psum | solution.py:9
  129.8 7.8 %copy-start.6 = (f32[256,1024]{1,0:T(8,128)S(1)}, f32[256,1024]{1,0:T(8,128)}, u32[]{:S(2)}) copy-start(f32[256,1024]{1,0:T(8,128)} %all-reduce.7.cloned.1.call-done) | copy-start | bytes 3145732
  135.6 2.0 copy-start.2
  137.7 1.0 copy-start.11
  141.8 51.3 %slice-start.1 = ((f32[1024,1024]{1,0:T(8,128)}), f32[768,1024]{1,0:T(8,128)S(1)}, s32[]{:S(2)}) async-start(f32[1024,1024]{1,0:T(8,128)} %copy-done.2), calls=%async_computation.7 | async-start | bytes 6291456 | tf_op jit(solution)/shard_map/slice | solution.py:48
  141.8 113.7 %all-reduce.11.cloned.1.call-start = ((), (), s32[]{:S(2)}) async-start(), calls=%async_computation.4 | async-start | bytes 2097152 | tf_op jit(solution)/shard_map/psum | solution.py:9
  193.1 7.8 %copy-start.9 = (f32[256,1024]{1,0:T(8,128)S(1)}, f32[256,1024]{1,0:T(8,128)}, u32[]{:S(2)}) copy-start(f32[256,1024]{1,0:T(8,128)} %all-reduce.9.cloned.1.call-done) | copy-start | bytes 3145732
  198.9 2.0 copy-start.1
  200.9 3.4 %copy-start.5 = (f32[256,1024]{1,0:T(8,128)S(1)}, f32[256,1024]{1,0:T(8,128)}, u32[]{:S(2)}) copy-start(f32[256,1024]{1,0:T(8,128)} %all-reduce.5.cloned.1.call-done) | copy-start | bytes 3145732
  204.2 7.2 %copy-start.7 = (f32[256,1024]{1,0:T(8,128)S(1)}, f32[256,1024]{1,0:T(8,128)}, u32[]{:S(2)}) copy-start(f32[256,1024]{1,0:T(8,128)} %all-reduce.7.cloned.1.call-done) | copy-start | bytes 3145732
  204.2 110.4 %reduce-scatter.2.cloned.1.call-start = ((), (), s32[]{:S(2)}) async-start(), calls=%async_computation.5 | async-start | bytes 4718592 | tf_op jit(solution)/shard_map/reduce_scatter | solution.py:57
  204.3 7.1 %copy-start = (f32[1024,1024]{1,0:T(8,128)S(1)}, f32[1024,1024]{1,0:T(8,128)}, u32[]{:S(2)}) copy-start(f32[1024,1024]{1,0:T(8,128)} %param.5) | copy-start | bytes 12582916
  211.4 4.8 %copy-start.10 = (f32[256,1024]{1,0:T(8,128)S(1)}, f32[256,1024]{1,0:T(8,128)}, u32[]{:S(2)}) copy-start(f32[256,1024]{1,0:T(8,128)} %all-reduce.9.cloned.1.call-done) | copy-start | bytes 3145732
  220.9 40.9 %copy-start.13 = (f32[1,256,1024]{2,1,0:T(8,128)S(1)}, f32[1,256,1024]{2,1,0:T(8,128)}, u32[]{:S(2)}) copy-start(f32[1,256,1024]{2,1,0:T(8,128)} %fusion.10) | copy-start | bytes 3145732
  220.9 40.9 %copy-start.14 = (f32[1,256,1024]{2,1,0:T(8,128)S(1)}, f32[1,256,1024]{2,1,0:T(8,128)}, u32[]{:S(2)}) copy-start(f32[1,256,1024]{2,1,0:T(8,128)} %fusion.8) | copy-start | bytes 3145732
  255.5 6.3 %copy-start.15 = (f32[1,256,1024]{2,1,0:T(8,128)S(1)}, f32[1,256,1024]{2,1,0:T(8,128)}, u32[]{:S(2)}) copy-start(f32[1,256,1024]{2,1,0:T(8,128)} %fusion.6) | copy-start | bytes 3145732
  264.1 1.9 slice-start
  264.1 2.2 copy-start.8
Sparse Core Ops, SparseCore 0:
  10.9 54.6 all-reduce.4
  78.6 51.1 all-reduce.6
  141.9 51.1 all-reduce.8
  204.3 51.1 all-reduce.10
  264.2 50.3 reduce-scatter.1
where the time goes:
time: 321 us
  waiting for transfers between devices  232 us (72%)
  matrix products  58.6 us (18%)
  between operations  14 us (4%)
  local copies, waits for them, and re-layouts  10.6 us (3%)
  other arithmetic  5.24 us (2%)
    psum x4, waiting for transfers between devices, broadcast(): return lax.psum(jnp.where(mine, array, jnp.zeros_like(array)), axis)  192 us
    reduce_scatter x1, waiting for transfers between devices, body(): lax.psum_scatter(jnp.stack(terms), 'col', scatter_dimension=1, tiled=True)  40.5 us
    dot_general x4, matrix products, body(): lax.dot_general(masked, solved, (((0,), (0,)), ((), ())), precision=hi, p...  23.3 us
    dot_general x4, matrix products, body(): lax.dot_general(solved, whitened, (((1,), (1,)), ((), ())), precision=hi,...  22.8 us
    dot_general x4, matrix products, body(): jnp.dot(diag_inverse[p].T, own, precision=hi, preferred_element_type=jnp....  12.5 us
    unnamed x32, local copies, waits for them, and re-layouts  8.3 us
  transfers between devices with their start and end apart: 5, of which 5 were waited for; matrix products, arithmetic and copies ran while one was open for 8% of the time, Pallas kernels for 0%

commit v1 on v0

v1 whole, which is shorter than its diff:
```python
import functools

import jax
import jax.numpy as jnp
from jax import lax
from jax.experimental import pallas as pl
from jax.experimental.pallas import tpu as pltpu
from jax.sharding import PartitionSpec as P

MESH = pl.DeviceIdType.MESH
CHUNK = 128
F32 = jnp.float32
BF16 = jnp.bfloat16


def split(x):
    hi = x.astype(BF16)
    return hi, (x - hi.astype(F32)).astype(BF16)


def product(a, b, dims):
    dot = functools.partial(lax.dot_general, dimension_numbers=(dims, ((), ())), preferred_element_type=F32)
    return dot(a[0], b[0]) + (dot(a[0], b[1]) + dot(a[1], b[0]))


NN = ((1,), (0,))
NT = ((1,), (1,))


def kernel(
    n_row, n_col, cot_ref, wht_ref, pan_ref, diag_ref, res_ref, out_ref,
    y, pth, ptl, dth, dtl, wh, wl, grad, rs_buf, recv_sem, down_sem, up_sem, rs_send, rs_recv,
):
    rows, rhs = cot_ref.shape
    panels, width = diag_ref.shape[0], diag_ref.shape[1]
    count = rhs // CHUNK
    blocks = rows // width
    tail = rows - width
    part = width // n_col
    row, col = lax.axis_index("row"), lax.axis_index("col")

    def down(p, c):
        return pltpu.make_async_remote_copy(
            src_ref=y.at[p, c], dst_ref=y.at[p, c], send_sem=down_sem.at[p, c], recv_sem=recv_sem.at[p, c],
            device_id={"row": lax.rem(row + n_row - 1, n_row)}, device_id_type=MESH,
        )

    def up(p, c):
        return pltpu.make_async_remote_copy(
            src_ref=y.at[p, c], dst_ref=y.at[p, c], send_sem=up_sem.at[p, c], recv_sem=recv_sem.at[p, c],
            device_id={"row": lax.rem(row + 1, n_row)}, device_id_type=MESH,
        )

    def scatter(p, j):
        peer = lax.rem(col + j, n_col)
        return pltpu.make_async_remote_copy(
            src_ref=grad.at[p, pl.ds(pl.multiple_of(peer * part, part), part)], dst_ref=rs_buf.at[p, j],
            send_sem=rs_send.at[p, j], recv_sem=rs_recv.at[p, j],
            device_id={"col": peer}, device_id_type=MESH,
        )

    def columns(c):
        return pl.ds(pl.multiple_of(c * CHUNK, CHUNK), CHUNK)

    def solve(p, c, own):
        y[p, c] = product((dth[p], dtl[p]), split(own), NN)

    barrier = pltpu.get_barrier_semaphore()
    for step in (1, n_row - 1):
        pl.semaphore_signal(barrier, inc=1, device_id={"row": lax.rem(row + step, n_row)}, device_id_type=MESH)
    for step in range(1, n_col):
        pl.semaphore_signal(barrier, inc=1, device_id={"col": lax.rem(col + step, n_col)}, device_id_type=MESH)

    @pl.loop(0, panels)
    def _(p):
        hi, lo = split(diag_ref[p].T)
        dth[p] = hi
        dtl[p] = lo

    pl.semaphore_wait(barrier, 2 + n_col - 1)

    @pl.when(row == n_row - 1)
    def _():
        @pl.loop(0, count)
        def _(c):
            solve(0, c, cot_ref[tail:, columns(c)])
            down(0, c).start()

    @pl.loop(0, panels)
    def _(p):
        for b in range(blocks):
            hi, lo = split(pan_ref[p, :, b * width : (b + 1) * width].T)
            pth[p, b * width : (b + 1) * width] = hi
            ptl[p, b * width : (b + 1) * width] = lo
        grad[p] = jnp.zeros(grad.shape[1:], F32)

    @pl.loop(0, count)
    def _(c):
        res_ref[:, columns(c)] = cot_ref[:, columns(c)]
        hi, lo = split(wht_ref[:, columns(c)])
        wh[c] = hi
        wl[c] = lo

    def reduce(p):
        total = grad[p, pl.ds(pl.multiple_of(col * part, part), part)]
        for j in range(1, n_col):
            scatter(p, j).wait_recv()
            total = total + rs_buf[p, j]
        out_ref[p] = total

    @pl.loop(0, panels)
    def _(p):
        root = n_row - 1 - p

        @pl.loop(0, count)
        def _(c):
            @pl.when(row != root)
            def _():
                down(p, c).wait_recv()

            @pl.when((row > root) & (row < n_row - 1))
            def _():
                up(p, c).start()

            @pl.when((row <= root) & (row > 0) & (root < n_row - 1) | (row < root) & (row > 0))
            def _():
                down(p, c).start()

            ys = split(y[p, c])

            @pl.when(row < root)
            def _():
                res_ref[tail:, columns(c)] -= product((pth[p, tail:], ptl[p, tail:]), ys, NN)

                @pl.when((row == root - 1) & (p + 1 < panels))
                def _():
                    solve(p + 1, c, res_ref[tail:, columns(c)])
                    up(p + 1, c).start()

            @pl.when(row == root)
            def _():
                res_ref[tail:, columns(c)] = y[p, c]

            for b in range(blocks - 1):
                at = slice(b * width, (b + 1) * width)
                res_ref[at, columns(c)] -= product((pth[p, at], ptl[p, at]), ys, NN)
            for b in range(blocks):
                at = slice(b * width, (b + 1) * width)
                grad[p, :, at] -= product(ys, (wh[c, at], wl[c, at]), NT)

        inner = lax.broadcasted_iota(jnp.int32, (width, width), 0)
        within = lax.broadcasted_iota(jnp.int32, (width, width), 1)
        keep = (row < root) | ((row == root) & (inner >= within))
        grad[p, :, tail:] = jnp.where(keep, grad[p, :, tail:], 0.0)
        for j in range(1, n_col):
            scatter(p, j).start()

        @pl.when(p > 0)
        def _():
            reduce(p - 1)

    reduce(panels - 1)

    @pl.loop(0, panels)
    def _(p):
        root = n_row - 1 - p
        for j in range(1, n_col):
            scatter(p, j).wait_send()

        @pl.loop(0, count)
        def _(c):
            @pl.when((row >= root) & (row < n_row - 1))
            def _():
                up(p, c).wait_send()

            @pl.when((row <= root) & (row > 0))
            def _():
                down(p, c).wait_send()


def solution(mesh):
    n_row, n_col = mesh.shape["row"], mesh.shape["col"]

    def body(cotangent, whitened, panel_rows, diag_inverse):
        rows, rhs = cotangent.shape
        panels, width = diag_inverse.shape[:2]
        assert panels <= n_row and n_row >= 3
        count = rhs // CHUNK
        vmem = pl.BlockSpec(memory_space=pltpu.VMEM)
        part = width // n_col
        return pl.pallas_call(
            functools.partial(kernel, n_row, n_col),
            out_shape=(
                jax.ShapeDtypeStruct((rows, rhs), F32),
                jax.ShapeDtypeStruct((panels, part, rows), F32),
            ),
            in_specs=[vmem] * 4,
            out_specs=(vmem, vmem),
            scratch_shapes=[
                pltpu.VMEM((panels, count, width, CHUNK), F32),
                pltpu.VMEM((panels, rows, width), BF16),
                pltpu.VMEM((panels, rows, width), BF16),
                pltpu.VMEM((panels, width, width), BF16),
                pltpu.VMEM((panels, width, width), BF16),
                pltpu.VMEM((count, rows, CHUNK), BF16),
                pltpu.VMEM((count, rows, CHUNK), BF16),
                pltpu.VMEM((panels, width, rows), F32),
                pltpu.VMEM((panels, n_col, part, rows), F32),
                pltpu.SemaphoreType.DMA((panels, count)),
                pltpu.SemaphoreType.DMA((panels, count)),
                pltpu.SemaphoreType.DMA((panels, count)),
                pltpu.SemaphoreType.DMA((panels, n_col)),
                pltpu.SemaphoreType.DMA((panels, n_col)),
            ],
            compiler_params=pltpu.CompilerParams(
                collective_id=0, has_side_effects=True, vmem_limit_bytes=60 * 1024 * 1024
            ),
        )(cotangent, whitened, panel_rows, diag_inverse)

    return jax.shard_map(
        body,
        mesh=mesh,
        in_specs=(P("row", "col"), P("row", "col"), P(None, None, "row"), P()),
        out_specs=(P("row", "col"), P(None, "col", "row")),
        check_vma=False,
    )
```

time: 321 us -> 127 us (0.40)
  the two profiles are of different devices: /device:TPU:0 before, /device:TPU:25 now
where the time goes in v1:
time: 127 us; the launch traced here: 126 us
  Pallas kernels  120 us (94%)
  local copies, waits for them, and re-layouts  5.64 us (4%)
    pallas_call x1, Pallas kernels, body(): pl.pallas_call(functools.partial(kernel, n_row, n_col), out_shape=(jax.Sh...  120 us
    unnamed x4, local copies, waits for them, and re-layouts  5.64 us

profile of v1, /device:TPU:25, one launch (start us, length us, event | category | flops | bytes accessed | tf_op | source)
XLA Modules:
  0.0 126.4 jit_solution(6694067946238780452)
XLA Ops:
  0.6 120.1 %shard_map.59 = (f32[1024,1024]{1,0:T(8,128)}, f32[4,32,1024]{2,1,0:T(8,128)}) custom-call(f32[1024,1024]{1,0:T(8,128)} %cot_ref.1, f32[1024,1024]{1,0:T(8,128)} %wht_ref.1, f32[4,256,1024]{2,1,0:T(8,128)} %pan_ref.1, f32[4,256,256]{2,1,0:T(8,128)} %diag_ref.1), custom_call_target="tpu_custom_call" | custom-call | tf_op jit(solution)/shard_map/pallas_call | solution.py:191
  120.7 0.0 copy-start
  120.7 4.8 %copy.8 = f32[1024,1024]{1,0:T(8,128)} copy(f32[1024,1024]{1,0:T(8,128)} %get-tuple-element.4) | data formatting | bytes 8388608
  125.6 0.0 copy-done
  125.6 0.8 copy.9
Async XLA Ops:
  120.7 4.9 %copy-start = (f32[4,32,1024]{2,1,0:T(8,128)S(1)}, f32[4,32,1024]{2,1,0:T(8,128)}, u32[]{:S(2)}) copy-start(f32[4,32,1024]{2,1,0:T(8,128)} %get-tuple-element.5) | copy-start | bytes 1572868

commit v2 on v1

v2 whole, which is shorter than its diff:
```python
import functools

import jax
import jax.numpy as jnp
from jax import lax
from jax.experimental import pallas as pl
from jax.experimental.pallas import tpu as pltpu
from jax.sharding import PartitionSpec as P

MESH = pl.DeviceIdType.MESH
CHUNK = 128
HALVES = 2
F32 = jnp.float32
BF16 = jnp.bfloat16


def split(x):
    hi = x.astype(BF16)
    return hi, (x - hi.astype(F32)).astype(BF16)


def product(a, b, dims):
    dot = functools.partial(lax.dot_general, dimension_numbers=(dims, ((), ())), preferred_element_type=F32)
    return dot(a[0], b[0]) + (dot(a[0], b[1]) + dot(a[1], b[0]))


NN = ((1,), (0,))
NT = ((1,), (1,))


def kernel(
    n_row, n_col, cot_hbm, wht_hbm, pan_hbm, diag_hbm, res_ref, out_ref,
    wht_ref, pan_ref, diag_ref, y, pth, ptl, dth, dtl, wh, wl, grad, rs_a, rs_b,
    local_sem, recv_sem, down_sem, up_sem, a_send, a_recv, b_send, b_recv,
):
    rows, rhs = res_ref.shape
    panels, width = diag_ref.shape[0], diag_ref.shape[1]
    count = rhs // CHUNK
    blocks = rows // width
    tail = rows - width
    part = width // n_col
    chips = n_col // 2
    half = width // HALVES
    row, col = lax.axis_index("row"), lax.axis_index("col")
    core, chip = lax.rem(col, 2), col // 2

    def y_copy(p, c, h, sems, step):
        block = y.at[p, c, h * half : (h + 1) * half]
        return pltpu.make_async_remote_copy(
            src_ref=block, dst_ref=block, send_sem=sems.at[p, c, h], recv_sem=recv_sem.at[p, c, h],
            device_id={"row": lax.rem(row + step, n_row)}, device_id_type=MESH,
        )

    def down(p, c, h):
        return y_copy(p, c, h, down_sem, n_row - 1)

    def up(p, c, h):
        return y_copy(p, c, h, up_sem, 1)

    def group(g):
        return slice(0, blocks - 1) if g == 0 else slice(blocks - 1, blocks)

    def pair_copy(p, m, g):
        place = (2 * m + 1 - core) * part
        return pltpu.make_async_remote_copy(
            src_ref=grad.at[p, group(g), pl.ds(pl.multiple_of(place, part), part)], dst_ref=rs_a.at[p, m, group(g)],
            send_sem=a_send.at[p, m, g], recv_sem=a_recv.at[p, m, g],
            device_id={"col": 2 * chip + 1 - core}, device_id_type=MESH,
        )

    def chip_copy(p, j, g):
        peer = lax.rem(chip + j, chips)
        return pltpu.make_async_remote_copy(
            src_ref=rs_a.at[p, peer, group(g)], dst_ref=rs_b.at[p, j, group(g)],
            send_sem=b_send.at[p, j, g], recv_sem=b_recv.at[p, j, g],
            device_id={"col": 2 * peer + core}, device_id_type=MESH,
        )

    def groups(p, act):
        act(0)

        @pl.when(row <= n_row - 1 - p)
        def _():
            act(1)

    def pair_start(p):
        def act(g):
            for m in range(chips):
                pair_copy(p, m, g).start()

        groups(p, act)

    def chip_start(p):
        def act(g):
            for m in range(chips):
                pair_copy(p, m, g).wait_recv()
            for m in range(chips):
                place = pl.multiple_of((2 * m + core) * part, part)
                rs_a[p, m, group(g)] += grad[p, group(g), pl.ds(place, part)]
            for j in range(1, chips):
                chip_copy(p, j, g).start()

        groups(p, act)

    def finish(p):
        def act(g):
            for j in range(1, chips):
                chip_copy(p, j, g).wait_recv()
            for b in range(blocks)[group(g)]:
                total = rs_a[p, chip, b]
                for j in range(1, chips):
                    total = total + rs_b[p, j, b]
                out_ref[p, :, b * width : (b + 1) * width] = total

        out_ref[p, :, tail:] = jnp.zeros((part, width), F32)
        groups(p, act)

    def columns(c):
        return pl.ds(pl.multiple_of(c * CHUNK, CHUNK), CHUNK)

    def solve(p, c, own):
        y[p, c] = product((dth[p], dtl[p]), split(own), NN)

    barrier = pltpu.get_barrier_semaphore()
    for step in (1, n_row - 1):
        pl.semaphore_signal(barrier, inc=1, device_id={"row": lax.rem(row + step, n_row)}, device_id_type=MESH)
    for step in range(1, n_col):
        pl.semaphore_signal(barrier, inc=1, device_id={"col": lax.rem(col + step, n_col)}, device_id_type=MESH)

    diag_copy = pltpu.make_async_copy(diag_hbm, diag_ref, local_sem.at[0])
    tail_copy = pltpu.make_async_copy(cot_hbm.at[tail:], res_ref.at[tail:], local_sem.at[1])
    pan_copy = pltpu.make_async_copy(pan_hbm, pan_ref, local_sem.at[2])
    head_copy = pltpu.make_async_copy(cot_hbm.at[:tail], res_ref.at[:tail], local_sem.at[3])
    wht_copy = pltpu.make_async_copy(wht_hbm, wht_ref, local_sem.at[4])
    for copy in (diag_copy, tail_copy, pan_copy, head_copy, wht_copy):
        copy.start()

    diag_copy.wait()

    @pl.loop(0, panels)
    def _(p):
        hi, lo = split(diag_ref[p].T)
        dth[p] = hi
        dtl[p] = lo

    tail_copy.wait()
    pl.semaphore_wait(barrier, 2 + n_col - 1)

    @pl.when(row == n_row - 1)
    def _():
        @pl.loop(0, count)
        def _(c):
            solve(0, c, res_ref[tail:, columns(c)])
            for h in range(HALVES):
                down(0, c, h).start()

    pan_copy.wait()

    @pl.loop(0, panels)
    def _(p):
        for b in range(blocks):
            hi, lo = split(pan_ref[p, :, b * width : (b + 1) * width].T)
            pth[p, b * width : (b + 1) * width] = hi
            ptl[p, b * width : (b + 1) * width] = lo
        grad[p] = jnp.zeros(grad.shape[1:], F32)

    head_copy.wait()
    wht_copy.wait()

    @pl.loop(0, count)
    def _(c):
        hi, lo = split(wht_ref[:, columns(c)])
        wh[c] = hi
        wl[c] = lo

    @pl.loop(0, panels)
    def _(p):
        root = n_row - 1 - p

        @pl.loop(0, count)
        def _(c):
            for h in range(HALVES):
                @pl.when(row != root)
                def _():
                    down(p, c, h).wait_recv()

                @pl.when((row > root) & (row < n_row - 1))
                def _():
                    up(p, c, h).start()

                @pl.when((row > 0) & ((row < root) | ((row == root) & (p > 0))))
                def _():
                    down(p, c, h).start()

            ys = split(y[p, c])

            @pl.when(row < root)
            def _():
                res_ref[tail:, columns(c)] -= product((pth[p, tail:], ptl[p, tail:]), ys, NN)

                @pl.when((row == root - 1) & (p + 1 < panels))
                def _():
                    solve(p + 1, c, res_ref[tail:, columns(c)])
                    for h in range(HALVES):
                        up(p + 1, c, h).start()

            @pl.when(row == root)
            def _():
                res_ref[tail:, columns(c)] = y[p, c]

            for b in range(blocks - 1):
                at = slice(b * width, (b + 1) * width)
                res_ref[at, columns(c)] -= product((pth[p, at], ptl[p, at]), ys, NN)
            for b in range(blocks):
                at = slice(b * width, (b + 1) * width)
                grad[p, b] -= product(ys, (wh[c, at], wl[c, at]), NT)

            @pl.when((c == count // 2) & (p > 0))
            def _():
                chip_start(p - 1)

        @pl.when(row == root)
        def _():
            inner = lax.broadcasted_iota(jnp.int32, (width, width), 0)
            within = lax.broadcasted_iota(jnp.int32, (width, width), 1)
            grad[p, blocks - 1] = jnp.where(inner >= within, grad[p, blocks - 1], 0.0)

        pair_start(p)

        @pl.when(p > 0)
        def _():
            finish(p - 1)

    chip_start(panels - 1)
    finish(panels - 1)

    @pl.loop(0, panels)
    def _(p):
        root = n_row - 1 - p

        def act(g):
            for m in range(chips):
                pair_copy(p, m, g).wait_send()
            for j in range(1, chips):
                chip_copy(p, j, g).wait_send()

        groups(p, act)

        @pl.loop(0, count)
        def _(c):
            for h in range(HALVES):
                @pl.when((row >= root) & (row < n_row - 1))
                def _():
                    up(p, c, h).wait_send()

                @pl.when((row <= root) & (row > 0))
                def _():
                    down(p, c, h).wait_send()


def solution(mesh):
    n_row, n_col = mesh.shape["row"], mesh.shape["col"]

    def body(cotangent, whitened, panel_rows, diag_inverse):
        rows, rhs = cotangent.shape
        panels, width = diag_inverse.shape[:2]
        assert panels <= n_row and n_row >= 3 and n_col % 2 == 0
        count, blocks, part, chips = rhs // CHUNK, rows // width, width // n_col, n_col // 2
        vmem = pl.BlockSpec(memory_space=pltpu.VMEM)
        hbm = pl.BlockSpec(memory_space=pltpu.HBM)
        dma = pltpu.SemaphoreType.DMA
        return pl.pallas_call(
            functools.partial(kernel, n_row, n_col),
            out_shape=(pltpu.VMEM((rows, rhs), F32), pltpu.VMEM((panels, part, rows), F32)),
            in_specs=[hbm] * 4,
            out_specs=(vmem, vmem),
            scratch_shapes=[
                pltpu.VMEM((rows, rhs), F32),
                pltpu.VMEM((panels, width, rows), F32),
                pltpu.VMEM((panels, width, width), F32),
                pltpu.VMEM((panels, count, width, CHUNK), F32),
                pltpu.VMEM((panels, rows, width), BF16),
                pltpu.VMEM((panels, rows, width), BF16),
                pltpu.VMEM((panels, width, width), BF16),
                pltpu.VMEM((panels, width, width), BF16),
                pltpu.VMEM((count, rows, CHUNK), BF16),
                pltpu.VMEM((count, rows, CHUNK), BF16),
                pltpu.VMEM((panels, blocks, width, width), F32),
                pltpu.VMEM((panels, chips, blocks, part, width), F32),
                pltpu.VMEM((panels, chips, blocks, part, width), F32),
                dma((5,)),
                dma((panels, count, HALVES)),
                dma((panels, count, HALVES)),
                dma((panels, count, HALVES)),
                dma((panels, chips, 2)),
                dma((panels, chips, 2)),
                dma((panels, chips, 2)),
                dma((panels, chips, 2)),
            ],
            compiler_params=pltpu.CompilerParams(
                collective_id=0, has_side_effects=True, vmem_limit_bytes=117 * 512 * 1024
            ),
        )(cotangent, whitened, panel_rows, diag_inverse)

    return jax.shard_map(
        body,
        mesh=mesh,
        in_specs=(P("row", "col"), P("row", "col"), P(None, None, "row"), P()),
        out_specs=(P("row", "col"), P(None, "col", "row")),
        check_vma=False,
    )
```

time: 127 us -> 109 us (0.86)
  the two profiles are of different devices: /device:TPU:25 before, /device:TPU:0 now
where the time goes in v2:
time: 109 us
  Pallas kernels  106 us (97%)
  local copies, waits for them, and re-layouts  2.81 us (3%)
    pallas_call x1, Pallas kernels, body(): pl.pallas_call(functools.partial(kernel, n_row, n_col), out_shape=(pltpu....  106 us
    unnamed x2, local copies, waits for them, and re-layouts  2.81 us

profile of v2, /device:TPU:0, one launch (start us, length us, event | category | flops | bytes accessed | tf_op | source)
XLA Modules:
  0.0 109.1 jit_solution(16652381620819640438)
XLA Ops:
  0.6 105.7 %shard_map.59 = (f32[1024,1024]{1,0:T(8,128)S(1)}, f32[4,32,1024]{2,1,0:T(8,128)S(1)}) custom-call(f32[1024,1024]{1,0:T(8,128)} %cot_hbm.1, f32[1024,1024]{1,0:T(8,128)} %wht_hbm.1, f32[4,256,1024]{2,1,0:T(8,128)} %pan_hbm.1, f32[4,256,256]{2,1,0:T(8,128)} %diag_hbm.1), custom_call_target="tpu_custom_call" | custom-call | tf_op jit(solution)/shard_map/pallas_call | solution.py:272
  106.3 2.0 %copy.8 = f32[1024,1024]{1,0:T(8,128)} copy(f32[1024,1024]{1,0:T(8,128)S(1)} %get-tuple-element.2) | data formatting | bytes 8388608
  108.3 0.8 copy.9

commit v3 on v2

--- a/solution.py
+++ b/solution.py
@@ -30,8 +30,8 @@
 
 def kernel(
     n_row, n_col, cot_hbm, wht_hbm, pan_hbm, diag_hbm, res_ref, out_ref,
-    wht_ref, pan_ref, diag_ref, y, pth, ptl, dth, dtl, wh, wl, grad, rs_a, rs_b,
-    local_sem, recv_sem, down_sem, up_sem, a_send, a_recv, b_send, b_recv,
+    wht_ref, pan_ref, diag_ref, y, pth, ptl, dth, dtl, wh, wl, grad, rs_a, rs_b, far_pan, far_own, far_sum, fph, fpl,
+    local_sem, recv_sem, down_sem, up_sem, a_send, a_recv, b_send, b_recv, fp_send, fp_recv, fo_send, fo_recv,
 ):
     rows, rhs = res_ref.shape
     panels, width = diag_ref.shape[0], diag_ref.shape[1]
@@ -43,6 +43,9 @@
     half = width // HALVES
     row, col = lax.axis_index("row"), lax.axis_index("col")
     core, chip = lax.rem(col, 2), col // 2
+    last = panels - 1
+    last_root = n_row - panels
+    helper = last_root + 1
 
     def y_copy(p, c, h, sems, step):
         block = y.at[p, c, h * half : (h + 1) * half]
@@ -56,6 +59,18 @@
 
     def up(p, c, h):
         return y_copy(p, c, h, up_sem, 1)
+
+    def far_panel(p):
+        return pltpu.make_async_remote_copy(
+            src_ref=pan_hbm.at[p, :, tail:], dst_ref=far_pan.at[p], send_sem=fp_send.at[p], recv_sem=fp_recv.at[p],
+            device_id={"row": lax.rem(row + 1, n_row)}, device_id_type=MESH,
+        )
+
+    def far_rows(c):
+        return pltpu.make_async_remote_copy(
+            src_ref=cot_hbm.at[tail:, columns(c)], dst_ref=far_own.at[c], send_sem=fo_send.at[c], recv_sem=fo_recv.at[c],
+            device_id={"row": lax.rem(row + 1, n_row)}, device_id_type=MESH,
+        )
 
     def group(g):
         return slice(0, blocks - 1) if g == 0 else slice(blocks - 1, blocks)
@@ -154,6 +169,16 @@
             for h in range(HALVES):
                 down(0, c, h).start()
 
+    @pl.when(row == last_root)
+    def _():
+        @pl.loop(0, last)
+        def _(p):
+            far_panel(p).start()
+
+        @pl.loop(0, count)
+        def _(c):
+            far_rows(c).start()
+
     pan_copy.wait()
 
     @pl.loop(0, panels)
@@ -173,18 +198,27 @@
         wh[c] = hi
         wl[c] = lo
 
+    far_sum[...] = jnp.zeros(far_sum.shape, F32)
+
     @pl.loop(0, panels)
     def _(p):
         root = n_row - 1 - p
 
+        @pl.when((row == helper) & (p < last))
+        def _():
+            far_panel(p).wait_recv()
+            hi, lo = split(far_pan[p].T)
+            fph[...] = hi
+            fpl[...] = lo
+
         @pl.loop(0, count)
         def _(c):
             for h in range(HALVES):
-                @pl.when(row != root)
+                @pl.when((row != root) & ((p < last) | (row != helper)))
                 def _():
                     down(p, c, h).wait_recv()
 
-                @pl.when((row > root) & (row < n_row - 1))
+                @pl.when((row > root) & (row < n_row - 1) & ((p < last) | (row != helper)))
                 def _():
                     up(p, c, h).start()
 
@@ -201,8 +235,22 @@
                 @pl.when((row == root - 1) & (p + 1 < panels))
                 def _():
                     solve(p + 1, c, res_ref[tail:, columns(c)])
+
+                    @pl.when(p + 1 < last)
+                    def _():
+                        for h in range(HALVES):
+                            up(p + 1, c, h).start()
+
+            @pl.when((row == helper) & (p < last))
+            def _():
+                far_sum[c] += product((fph[...], fpl[...]), ys, NN)
+
+                @pl.when(p == last - 1)
+                def _():
+                    far_rows(c).wait_recv()
+                    solve(last, c, far_own[c] - far_sum[c])
                     for h in range(HALVES):
-                        up(p + 1, c, h).start()
+                        up(last, c, h).start()
 
             @pl.when(row == root)
             def _():
@@ -249,13 +297,23 @@
         @pl.loop(0, count)
         def _(c):
             for h in range(HALVES):
-                @pl.when((row >= root) & (row < n_row - 1))
+                @pl.when((row >= root) & (row < n_row - 1) & ((p < last) | (row > last_root)))
                 def _():
                     up(p, c, h).wait_send()
 
                 @pl.when((row <= root) & (row > 0))
                 def _():
                     down(p, c, h).wait_send()
+
+    @pl.when(row == last_root)
+    def _():
+        @pl.loop(0, last)
+        def _(p):
+            far_panel(p).wait_send()
+
+        @pl.loop(0, count)
+        def _(c):
+            far_rows(c).wait_send()
 
 
 def solution(mesh):
@@ -264,7 +322,7 @@
     def body(cotangent, whitened, panel_rows, diag_inverse):
         rows, rhs = cotangent.shape
         panels, width = diag_inverse.shape[:2]
-        assert panels <= n_row and n_row >= 3 and n_col % 2 == 0
+        assert 3 <= panels <= n_row and n_col % 2 == 0
         count, blocks, part, chips = rhs // CHUNK, rows // width, width // n_col, n_col // 2
         vmem = pl.BlockSpec(memory_space=pltpu.VMEM)
         hbm = pl.BlockSpec(memory_space=pltpu.HBM)
@@ -288,6 +346,11 @@
                 pltpu.VMEM((panels, blocks, width, width), F32),
                 pltpu.VMEM((panels, chips, blocks, part, width), F32),
                 pltpu.VMEM((panels, chips, blocks, part, width), F32),
+                pltpu.VMEM((panels - 1, width, width), F32),
+                pltpu.VMEM((count, width, CHUNK), F32),
+                pltpu.VMEM((count, width, CHUNK), F32),
+                pltpu.VMEM((width, width), BF16),
+                pltpu.VMEM((width, width), BF16),
                 dma((5,)),
                 dma((panels, count, HALVES)),
                 dma((panels, count, HALVES)),
@@ -296,6 +359,10 @@
                 dma((panels, chips, 2)),
                 dma((panels, chips, 2)),
                 dma((panels, chips, 2)),
+                dma((panels - 1,)),
+                dma((panels - 1,)),
+                dma((count,)),
+                dma((count,)),
             ],
             compiler_params=pltpu.CompilerParams(
                 collective_id=0, has_side_effects=True, vmem_limit_bytes=117 * 512 * 1024

time: 109 us -> 110 us (level)
  no operation moved by 1% of the time
where the time goes in v3:
time: 110 us
  Pallas kernels  106 us (96%)
  local copies, waits for them, and re-layouts  2.81 us (3%)
    pallas_call x1, Pallas kernels, body(): pl.pallas_call(functools.partial(kernel, n_row, n_col), out_shape=(pltpu....  106 us
    unnamed x2, local copies, waits for them, and re-layouts  2.81 us

profile of v3, /device:TPU:0, one launch (start us, length us, event | category | flops | bytes accessed | tf_op | source)
XLA Modules:
  0.0 109.7 jit_solution(2997108685729110550)
XLA Ops:
  0.6 106.3 %shard_map.59 = (f32[1024,1024]{1,0:T(8,128)S(1)}, f32[4,32,1024]{2,1,0:T(8,128)S(1)}) custom-call(f32[1024,1024]{1,0:T(8,128)} %cot_hbm.1, f32[1024,1024]{1,0:T(8,128)} %wht_hbm.1, f32[4,256,1024]{2,1,0:T(8,128)} %pan_hbm.1, f32[4,256,256]{2,1,0:T(8,128)} %diag_hbm.1), custom_call_target="tpu_custom_call" | custom-call | tf_op jit(solution)/shard_map/pallas_call | solution.py:330
  106.9 2.0 %copy.8 = f32[1024,1024]{1,0:T(8,128)} copy(f32[1024,1024]{1,0:T(8,128)S(1)} %get-tuple-element.2) | data formatting | bytes 8388608
  108.9 0.8 copy.9

commit v4 on v3

--- a/solution.py
+++ b/solution.py
@@ -147,17 +147,15 @@
     pan_copy = pltpu.make_async_copy(pan_hbm, pan_ref, local_sem.at[2])
     head_copy = pltpu.make_async_copy(cot_hbm.at[:tail], res_ref.at[:tail], local_sem.at[3])
     wht_copy = pltpu.make_async_copy(wht_hbm, wht_ref, local_sem.at[4])
-    for copy in (diag_copy, tail_copy, pan_copy, head_copy, wht_copy):
-        copy.start()
-
-    diag_copy.wait()
-
-    @pl.loop(0, panels)
-    def _(p):
+    def inverse(p):
         hi, lo = split(diag_ref[p].T)
         dth[p] = hi
         dtl[p] = lo
 
+    diag_copy.start()
+    tail_copy.start()
+    diag_copy.wait()
+    inverse(0)
     tail_copy.wait()
     pl.semaphore_wait(barrier, 2 + n_col - 1)
 
@@ -179,6 +177,13 @@
         def _(c):
             far_rows(c).start()
 
+    for copy in (pan_copy, wht_copy, head_copy):
+        copy.start()
+
+    @pl.loop(1, panels)
+    def _(p):
+        inverse(p)
+
     pan_copy.wait()
 
     @pl.loop(0, panels)
@@ -256,12 +261,18 @@
             def _():
                 res_ref[tail:, columns(c)] = y[p, c]
 
-            for b in range(blocks - 1):
-                at = slice(b * width, (b + 1) * width)
-                res_ref[at, columns(c)] -= product((pth[p, at], ptl[p, at]), ys, NN)
-            for b in range(blocks):
-                at = slice(b * width, (b + 1) * width)
-                grad[p, b] -= product(ys, (wh[c, at], wl[c, at]), NT)
+            begin = jnp.where((row == last_root) & (p == last), panels, p)
+            end = jnp.where((row == last_root) & (p == last - 1), panels, p + 1)
+
+            @pl.loop(begin, end)
+            def _(q):
+                yq = split(y[q, c])
+                for b in range(blocks - 1):
+                    at = slice(b * width, (b + 1) * width)
+                    res_ref[at, columns(c)] -= product((pth[q, at], ptl[q, at]), yq, NN)
+                for b in range(blocks):
+                    at = slice(b * width, (b + 1) * width)
+                    grad[q, b] -= product(yq, (wh[c, at], wl[c, at]), NT)
 
             @pl.when((c == count // 2) & (p > 0))
             def _():
@@ -275,12 +286,13 @@
 
         pair_start(p)
 
-        @pl.when(p > 0)
+        @pl.when((p > 0) & (p < last))
         def _():
             finish(p - 1)
 
-    chip_start(panels - 1)
-    finish(panels - 1)
+    chip_start(last)
+    finish(last - 1)
+    finish(last)
 
     @pl.loop(0, panels)
     def _(p):
@@ -314,6 +326,17 @@
         @pl.loop(0, count)
         def _(c):
             far_rows(c).wait_send()
+
+
+def store_kernel(res_ref, grad_ref, res_hbm, grad_hbm, sems):
+    copies = (
+        pltpu.make_async_copy(res_ref, res_hbm, sems.at[0]),
+        pltpu.make_async_copy(grad_ref, grad_hbm, sems.at[1]),
+    )
+    for copy in copies:
+        copy.start()
+    for copy in copies:
+        copy.wait()
 
 
 def solution(mesh):
@@ -327,7 +350,7 @@
         vmem = pl.BlockSpec(memory_space=pltpu.VMEM)
         hbm = pl.BlockSpec(memory_space=pltpu.HBM)
         dma = pltpu.SemaphoreType.DMA
-        return pl.pallas_call(
+        kept = pl.pallas_call(
             functools.partial(kernel, n_row, n_col),
             out_shape=(pltpu.VMEM((rows, rhs), F32), pltpu.VMEM((panels, part, rows), F32)),
             in_specs=[hbm] * 4,
@@ -368,6 +391,14 @@
                 collective_id=0, has_side_effects=True, vmem_limit_bytes=117 * 512 * 1024
             ),
         )(cotangent, whitened, panel_rows, diag_inverse)
+        return pl.pallas_call(
+            store_kernel,
+            out_shape=tuple(jax.ShapeDtypeStruct(k.shape, F32) for k in kept),
+            in_specs=[pl.BlockSpec(memory_space=pl.ANY)] * 2,
+            out_specs=(hbm, hbm),
+            scratch_shapes=[dma((2,))],
+            compiler_params=pltpu.CompilerParams(vmem_limit_bytes=1024 * 1024),
+        )(*kept)
 
     return jax.shard_map(
         body,

time: 110 us -> 106 us (0.964)
  local copies, waits for them, and re-layouts: 2.81 us -> 0 us
    pallas_call x1, Pallas kernels: 106 us -> 103 us  [body(): pl.pallas_call(functools.partial(kernel, n_row, n_col), out_shape=(pltpu....]
    unnamed x2 -> x0, local copies, waits for them, and re-layouts: 2.81 us -> none
    pallas_call x0 -> x1, Pallas kernels: none -> 2.19 us  [body(): pl.pallas_call(store_kernel, out_shape=tuple((jax.ShapeDtypeStruct(k.shap...]
where the time goes in v4:
time: 106 us
  Pallas kernels  105 us (99%)
    pallas_call x1, Pallas kernels, body(): pl.pallas_call(functools.partial(kernel, n_row, n_col), out_shape=(pltpu....  103 us
    pallas_call x1, Pallas kernels, body(): pl.pallas_call(store_kernel, out_shape=tuple((jax.ShapeDtypeStruct(k.shap...  2.19 us

profile of v4, /device:TPU:0, one launch (start us, length us, event | category | flops | bytes accessed | tf_op | source)
XLA Modules:
  0.0 106.1 jit_solution(8189176966563102371)
XLA Ops:
  0.6 103.2 %shard_map.59 = (f32[1024,1024]{1,0:T(8,128)S(1)}, f32[4,32,1024]{2,1,0:T(8,128)S(1)}) custom-call(f32[1024,1024]{1,0:T(8,128)} %cot_hbm.1, f32[1024,1024]{1,0:T(8,128)} %wht_hbm.1, f32[4,256,1024]{2,1,0:T(8,128)} %pan_hbm.1, f32[4,256,256]{2,1,0:T(8,128)} %diag_hbm.1), custom_call_target="tpu_custom_call" | custom-call | tf_op jit(solution)/shard_map/pallas_call | solution.py:353
  103.9 2.2 %shard_map.60 = (f32[1024,1024]{1,0:T(8,128)}, f32[4,32,1024]{2,1,0:T(8,128)}) custom-call(f32[1024,1024]{1,0:T(8,128)S(1)} %get-tuple-element.4.res_ref, f32[4,32,1024]{2,1,0:T(8,128)S(1)} %get-tuple-element.5.grad_ref), custom_call_target="tpu_custom_call" | custom-call | tf_op jit(solution)/shard_map/pallas_call | solution.py:394

commit v5 on v4

--- a/solution.py
+++ b/solution.py
@@ -227,9 +227,18 @@
                 def _():
                     up(p, c, h).start()
 
-                @pl.when((row > 0) & ((row < root) | ((row == root) & (p > 0))))
+                @pl.when((row > 0) & (row < root))
                 def _():
                     down(p, c, h).start()
+
+            next_root = (row == root - 1) & (p < last)
+
+            @pl.when(next_root & (row > 0) & (c == count - 1))
+            def _():
+                @pl.loop(0, count - 1)
+                def _(k):
+                    for h in range(HALVES):
+                        down(p + 1, k, h).start()
 
             ys = split(y[p, c])
 
@@ -237,9 +246,14 @@
             def _():
                 res_ref[tail:, columns(c)] -= product((pth[p, tail:], ptl[p, tail:]), ys, NN)
 
-                @pl.when((row == root - 1) & (p + 1 < panels))
+                @pl.when(next_root)
                 def _():
                     solve(p + 1, c, res_ref[tail:, columns(c)])
+
+                    @pl.when((row > 0) & (c == count - 1))
+                    def _():
+                        for h in range(HALVES):
+                            down(p + 1, c, h).start()
 
                     @pl.when(p + 1 < last)
                     def _():
@@ -278,6 +292,10 @@
             def _():
                 chip_start(p - 1)
 
+                @pl.when((p > 1) & (p < last))
+                def _():
+                    finish(p - 2)
+
         @pl.when(row == root)
         def _():
             inner = lax.broadcasted_iota(jnp.int32, (width, width), 0)
@@ -286,13 +304,9 @@
 
         pair_start(p)
 
-        @pl.when((p > 0) & (p < last))
-        def _():
-            finish(p - 1)
-
     chip_start(last)
-    finish(last - 1)
-    finish(last)
+    for p in range(last - 2, panels):
+        finish(p)
 
     @pl.loop(0, panels)
     def _(p):

time: 106 us -> 107 us (level)
  no operation moved by 1% of the time
where the time goes in v5:
time: 107 us
  Pallas kernels  106 us (99%)
    pallas_call x1, Pallas kernels, body(): pl.pallas_call(functools.partial(kernel, n_row, n_col), out_shape=(pltpu....  104 us
    pallas_call x1, Pallas kernels, body(): pl.pallas_call(store_kernel, out_shape=tuple((jax.ShapeDtypeStruct(k.shap...  2.19 us

profile of v5, /device:TPU:0, one launch (start us, length us, event | category | flops | bytes accessed | tf_op | source)
XLA Modules:
  0.0 106.6 jit_solution(4691771201194239361)
XLA Ops:
  0.6 103.7 %shard_map.59 = (f32[1024,1024]{1,0:T(8,128)S(1)}, f32[4,32,1024]{2,1,0:T(8,128)S(1)}) custom-call(f32[1024,1024]{1,0:T(8,128)} %cot_hbm.1, f32[1024,1024]{1,0:T(8,128)} %wht_hbm.1, f32[4,256,1024]{2,1,0:T(8,128)} %pan_hbm.1, f32[4,256,256]{2,1,0:T(8,128)} %diag_hbm.1), custom_call_target="tpu_custom_call" | custom-call | tf_op jit(solution)/shard_map/pallas_call | solution.py:367
  104.4 2.2 %shard_map.60 = (f32[1024,1024]{1,0:T(8,128)}, f32[4,32,1024]{2,1,0:T(8,128)}) custom-call(f32[1024,1024]{1,0:T(8,128)S(1)} %get-tuple-element.4.res_ref, f32[4,32,1024]{2,1,0:T(8,128)S(1)} %get-tuple-element.5.grad_ref), custom_call_target="tpu_custom_call" | custom-call | tf_op jit(solution)/shard_map/pallas_call | solution.py:408
